TPU v7x, 256 devices: a whole 4x4x8 slice. The times are simulated.
256 devices in a mesh: row: 16 (over z, x_lo), col: 16 (over y, x_hi, core).
Axes of the slice: x: 4 (x_hi: 2, x_lo: 2; x = x_hi * 2 + x_lo), y: 4, z: 8, core: 2. Of those that a mesh axis runs over, the one named last changes fastest.
Arguments:
- pair: bfloat16 [512, 512, 128], P('row', 'col'), may hold values from -6 to 6
- pair_mask: int32 [512, 512], P('row', 'col'), may hold values from 0 to 1, as said below
- proj_weight: bfloat16 [128, 640], replicated, may hold values from -0.5 to 0.5
- out_weight: bfloat16 [128, 128], replicated, may hold values from -0.5 to 0.5
- in_gain: float32 [128], replicated, may hold values from 0.5 to 1.5
- out_gain: float32 [128], replicated, may hold values from 0.5 to 1.5
- cotangent: bfloat16 [512, 512, 128], P('row', 'col'), may hold values from -6 to 6
Outputs:
- d_pair: float32 [512, 512, 128], P('row', 'col')
- d_proj_weight: float32 [128, 640], replicated
- d_out_weight: float32 [128, 128], replicated
- d_in_gain: float32 [128], replicated
- d_out_gain: float32 [128], replicated
Inputs may be any that keep to these rules, and one draw needn't show every extreme that they name: pair_mask[i, j] is the product of a 0/1 flag of token i and the same flag of token j.
All inputs are finite; a program needn't handle non-finite values.
Results may differ from a plain program's by a relative error of at most 0.019.
Values may be sent and summed in bfloat16 or wider, within the bound.
A program may use at most 128 MiB of HBM per device.

v0:
```python
import jax
import jax.numpy as jnp
from jax import lax
from jax.sharding import PartitionSpec as P


def normalize(values):
    average = jnp.mean(values, axis=-1, keepdims=True)
    centred = values - average
    spread = jnp.mean(centred * centred, axis=-1, keepdims=True)
    inverse = lax.rsqrt(spread + 1e-05)
    return (centred * inverse, inverse)


def layer_back(grad_hat, normed, inverse):
    first_mean = jnp.mean(grad_hat, axis=-1, keepdims=True)
    second_mean = jnp.mean(grad_hat * normed, axis=-1, keepdims=True)
    return (grad_hat - first_mean - normed * second_mean) * inverse


AXES = ("row", "col")


def exchange(x):
    return lax.all_to_all(x, AXES, split_axis=0, concat_axis=0, tiled=True)


def body(pair, pair_mask, proj_weight, out_weight, in_gain, out_gain, cotangent):
    t = pair.shape[0]
    half_t = t // 2
    channels = pair.shape[2]
    rows = lax.axis_size("row")
    cols = lax.axis_size("col")
    total = t * rows
    half = lax.rem(lax.axis_index("col"), 2)
    normed, inverse = normalize(pair.astype(jnp.float32))
    zn = (normed * in_gain).astype(jnp.bfloat16)
    linear = jnp.einsum("ijc,ce->ije", zn, proj_weight, preferred_element_type=jnp.float32)
    proj_left = linear[..., 0:channels]
    gate_left = linear[..., channels : 2 * channels]
    proj_right = linear[..., 2 * channels : 3 * channels]
    gate_right = linear[..., 3 * channels : 4 * channels]
    gate_out = linear[..., 4 * channels :]
    mask_f = pair_mask.astype(jnp.float32)[..., None]
    sig_left = jax.nn.sigmoid(gate_left)
    sig_right = jax.nn.sigmoid(gate_right)
    left = (mask_f * sig_left * proj_left).astype(jnp.bfloat16)
    right = (mask_f * sig_right * proj_right).astype(jnp.bfloat16)

    def out_full(x):
        x = jnp.transpose(x, (2, 0, 1)).reshape(channels, 1, t * t)
        return jnp.broadcast_to(x, (channels, 2, t * t)).reshape(2 * channels, t * t)

    def matrix(x):
        return x.reshape(rows, cols, t, t).transpose(0, 2, 1, 3).reshape(rows * t, cols * t)

    def pick(x):
        x = x.reshape(x.shape[0], -1, 2, half_t)
        return lax.dynamic_index_in_dim(x, half, 2, keepdims=False).reshape(x.shape[0], -1)

    sent = exchange(jnp.concatenate([out_full(left), out_full(right)], axis=1))
    left_c = matrix(sent[:, : t * t])
    right_c = matrix(sent[:, t * t :])
    tri_c = jnp.einsum("ki,kj->ij", pick(left_c), right_c, preferred_element_type=jnp.float32)
    tri_c = tri_c.astype(jnp.bfloat16).reshape(rows, half_t, cols, t).transpose(0, 2, 1, 3)
    tri = exchange(tri_c.reshape(rows * cols, half_t * t))
    triangle = tri.reshape(channels, 2 * half_t, t).transpose(1, 2, 0).astype(jnp.float32)
    tri_hat, tri_inv = normalize(triangle)
    onorm = (tri_hat * out_gain).astype(jnp.bfloat16)
    projected = jnp.einsum("ijc,cd->ijd", onorm, out_weight, preferred_element_type=jnp.float32)
    sig_gate = jax.nn.sigmoid(gate_out)
    cot_f = cotangent.astype(jnp.float32)
    dproj = (cot_f * sig_gate).astype(jnp.bfloat16)
    dgate = cot_f * projected * sig_gate * (1.0 - sig_gate)
    out_weight_local = jnp.einsum("ijc,ijd->cd", onorm, dproj, preferred_element_type=jnp.float32)
    donorm = jnp.einsum("ijd,cd->ijc", dproj, out_weight, preferred_element_type=jnp.float32)
    out_gain_local = jnp.sum(donorm * tri_hat, axis=(0, 1))
    dtri = layer_back(donorm * out_gain, tri_hat, tri_inv).astype(jnp.bfloat16)
    dtri_c = matrix(exchange(out_full(dtri)))
    dtri_rows = lax.dynamic_index_in_dim(
        dtri_c.reshape(rows, 2, half_t, cols * t), half, 1, keepdims=False
    ).reshape(rows * half_t, cols * t)
    dleft_c = jnp.einsum("kj,ij->ki", right_c, dtri_rows, preferred_element_type=jnp.float32)
    dright_c = jnp.einsum("ki,ij->kj", left_c, pick(dtri_c), preferred_element_type=jnp.float32)

    def back(x):
        x = x.astype(jnp.bfloat16).reshape(rows, t, cols, half_t)
        return x.transpose(0, 2, 1, 3).reshape(rows * cols, t * half_t)

    grads = exchange(jnp.concatenate([back(dleft_c), back(dright_c)], axis=1))

    def cells(x):
        x = x.reshape(channels, 2, t, half_t).transpose(2, 1, 3, 0)
        return x.reshape(t, t, channels).astype(jnp.float32)

    dleft = cells(grads[:, : t * half_t])
    dright = cells(grads[:, t * half_t :])
    dlin = jnp.concatenate(
        [
            dleft * mask_f * sig_left,
            dleft * mask_f * proj_left * sig_left * (1.0 - sig_left),
            dright * mask_f * sig_right,
            dright * mask_f * proj_right * sig_right * (1.0 - sig_right),
            dgate,
        ],
        axis=-1,
    ).astype(jnp.bfloat16)
    proj_local = jnp.einsum("ijc,ije->ce", zn, dlin, preferred_element_type=jnp.float32)
    dzn = jnp.einsum("ije,ce->ijc", dlin, proj_weight, preferred_element_type=jnp.float32)
    in_gain_local = jnp.sum(dzn * normed, axis=(0, 1))
    d_pair = layer_back(dzn * in_gain, normed, inverse)
    proj_sum, out_weight_sum, in_gain_sum, out_gain_sum = lax.psum(
        (proj_local, out_weight_local, in_gain_local, out_gain_local), ("row", "col")
    )
    return (
        d_pair,
        proj_sum / total,
        out_weight_sum / total,
        in_gain_sum / total,
        out_gain_sum / total,
    )


def solution(mesh):
    in_specs = (P("row", "col", None), P("row", "col"), P(), P(), P(), P(), P("row", "col", None))
    out_specs = (P("row", "col", None), P(), P(), P(), P())
    return jax.shard_map(body, mesh=mesh, in_specs=in_specs, out_specs=out_specs, check_vma=False)
```

profile of v0, /device:TPU:1, one launch (start us, length us, event | category | flops | bytes accessed | tf_op | source)
XLA Modules:
  0.0 653.1 jit_solution(1382171473351890345)
XLA Ops:
  28.2 17.0 %all-to-all-start = ((bf16[256,2,1024]{2,1,0:T(2,128)(2,1)}), bf16[256,2,1024]{2,1,0:T(2,128)(2,1)}, u32[]{:S(2)}, u32[]{:S(2)}) async-start(bf16[256,2,1024]{2,1,0:T(2,128)(2,1)} %reshape.165), calls=%async_computation | async-start | bytes 2097152 | tf_op jit(solution)/shard_map/all_to_all | solution.py:25
  45.2 31.4 %all-to-all-done = bf16[256,2,1024]{2,1,0:T(2,128)(2,1)} async-done(((bf16[256,2,1024]{2,1,0:T(2,128)(2,1)}), bf16[256,2,1024]{2,1,0:T(2,128)(2,1)}, u32[]{:S(2)}, u32[]{:S(2)}) %all-to-all-start) | async-done | bytes 1048608 | tf_op jit(solution)/shard_map/all_to_all | solution.py:25
  76.7 7.5 %reshape.166 = bf16[256,1,2048]{2,1,0:T(2,128)(2,1)} reshape(bf16[256,2,1024]{2,1,0:T(2,128)(2,1)} %all-to-all-done) | data formatting | bytes 2097152
  100.9 4.4 copy.69
  105.3 4.1 reshape_reshape.9
  123.0 20.4 %all_to_all.44 = bf16[256,2,256]{2,1,0:T(2,128)(2,1)S(1)} all-to-all(bf16[256,2,256]{2,1,0:T(2,128)(2,1)S(1)} %reshape.167), channel_id=1, replica_groups=mesh['row'=16,'col'=16] {'row','col'}, dimensions={0} | all-to-all | bytes 524288 | tf_op jit(solution)/shard_map/all_to_all | solution.py:25
  158.8 4.3 all_to_all.39
  163.2 5.6 reduce.5
  171.0 7.2 %all-to-all-start.2 = ((bf16[256,2,512]{2,1,0:T(2,128)(2,1)}), bf16[256,2,512]{2,1,0:T(2,128)(2,1)}, u32[]{:S(2)}, u32[]{:S(2)}) async-start(bf16[256,2,512]{2,1,0:T(2,128)(2,1)} %reshape.169), calls=%async_computation.2 | async-start | bytes 1048576 | tf_op jit(solution)/shard_map/all_to_all | solution.py:25
  182.0 4.1 reshape.149
  186.1 12.2 %all-to-all-done.2 = bf16[256,2,512]{2,1,0:T(2,128)(2,1)} async-done(((bf16[256,2,512]{2,1,0:T(2,128)(2,1)}), bf16[256,2,512]{2,1,0:T(2,128)(2,1)}, u32[]{:S(2)}, u32[]{:S(2)}) %all-to-all-start.2) | async-done | bytes 524320 | tf_op jit(solution)/shard_map/all_to_all | solution.py:25
  198.3 4.4 reshape.170
  202.7 4.9 reduce.1
  211.4 4.4 copy.80
  219.6 4.1 reshape_reshape.11
  245.6 5.1 reshape.152
  253.7 5.1 reshape.148
  265.6 6.8 %all-to-all-start.3 = ((bf16[256,2,512]{2,1,0:T(2,128)(2,1)}), bf16[256,2,512]{2,1,0:T(2,128)(2,1)}, u32[]{:S(2)}, u32[]{:S(2)}) async-start(bf16[256,2,512]{2,1,0:T(2,128)(2,1)} %reshape.171), calls=%async_computation.3 | async-start | bytes 1048576 | tf_op jit(solution)/shard_map/all_to_all | solution.py:25
  274.6 17.4 %all-to-all-done.3 = bf16[256,2,512]{2,1,0:T(2,128)(2,1)} async-done(((bf16[256,2,512]{2,1,0:T(2,128)(2,1)}), bf16[256,2,512]{2,1,0:T(2,128)(2,1)}, u32[]{:S(2)}, u32[]{:S(2)}) %all-to-all-start.3) | async-done | bytes 524320 | tf_op jit(solution)/shard_map/all_to_all | solution.py:25
  292.1 4.6 reshape.172
  302.9 4.5 copy.85
  311.1 4.5 copy.84
  323.3 72.4 %all-reduce = (f32[128]{0:T(128)S(1)}, f32[128]{0:T(128)S(1)}) all-reduce(f32[128]{0:T(128)S(1)} %get-tuple-element.7, f32[128]{0:T(128)S(1)} %get-tuple-element.5), channel_id=1, replica_groups=mesh['row'=16,'col'=16] {'row','col'}, use_global_device_ids=true, to_apply=%region_11.12 | all-reduce | flops 256 | bytes 2048 | tf_op jit(solution)/shard_map/psum | solution.py:112
  398.2 244.6 %all-reduce.4.cloned.1.call-done = (f32[128,640]{1,0:T(8,128)}, f32[128,128]{1,0:T(8,128)}) async-done(((f32[128,640]{1,0:T(8,128)}, f32[128,128]{1,0:T(8,128)}), (f32[128,640]{1,0:T(8,128)}, f32[128,128]{1,0:T(8,128)})) %all-reduce.4.cloned.1.call-update) | async-done | bytes 393232 | tf_op jit(solution)/shard_map/psum | solution.py:112
  (103 shorter events, 137.3 us)
Async XLA Ops:
  7.2 3.3 copy-start
  7.2 4.9 copy-start.5
  28.2 48.5 %all-to-all-start = ((bf16[256,2,1024]{2,1,0:T(2,128)(2,1)}), bf16[256,2,1024]{2,1,0:T(2,128)(2,1)}, u32[]{:S(2)}, u32[]{:S(2)}) async-start(bf16[256,2,1024]{2,1,0:T(2,128)(2,1)} %reshape.165), calls=%async_computation | async-start | bytes 2097152 | tf_op jit(solution)/shard_map/all_to_all | solution.py:25
  96.9 13.4 %copy-start.3 = (bf16[512,512]{1,0:T(8,128)(2,1)}, bf16[512,512]{1,0:T(8,128)(2,1)S(1)}, u32[]{:S(2)}) copy-start(bf16[512,512]{1,0:T(8,128)(2,1)S(1)} %reshape.141) | copy-start | bytes 1572868
  148.8 3.3 copy-start.7
  148.8 3.3 copy-start.9
  171.0 27.3 %all-to-all-start.2 = ((bf16[256,2,512]{2,1,0:T(2,128)(2,1)}), bf16[256,2,512]{2,1,0:T(2,128)(2,1)}, u32[]{:S(2)}, u32[]{:S(2)}) async-start(bf16[256,2,512]{2,1,0:T(2,128)(2,1)} %reshape.169), calls=%async_computation.2 | async-start | bytes 1048576 | tf_op jit(solution)/shard_map/all_to_all | solution.py:25
  265.6 26.4 %all-to-all-start.3 = ((bf16[256,2,512]{2,1,0:T(2,128)(2,1)}), bf16[256,2,512]{2,1,0:T(2,128)(2,1)}, u32[]{:S(2)}, u32[]{:S(2)}) async-start(bf16[256,2,512]{2,1,0:T(2,128)(2,1)} %reshape.171), calls=%async_computation.3 | async-start | bytes 1048576 | tf_op jit(solution)/shard_map/all_to_all | solution.py:25
  272.4 370.4 %all-reduce.4.cloned.1.call-start = ((), (), s32[]{:S(2)}) async-start(), calls=%async_computation.4 | async-start | bytes 786432 | tf_op jit(solution)/shard_map/psum | solution.py:112
  317.2 1.0 copy-start.6
  317.4 2.3 copy-start.1
  317.4 2.3 copy-start.8
  318.7 1.1 copy-start.4
  319.8 76.6 %copy-start.2 = (bf16[32,32,128]{2,1,0:T(8,128)(2,1)S(1)}, bf16[32,32,128]{2,1,0:T(8,128)(2,1)}, u32[]{:S(2)}) copy-start(bf16[32,32,128]{2,1,0:T(8,128)(2,1)} %param.7) | copy-start | bytes 786436
Sparse Core Ops, SparseCore 0:
  396.4 246.3 all-reduce.3
where the time goes:
time: 660 us; the launch traced here: 653 us
  waiting for transfers between devices  306 us (46%)
  local copies, waits for them, and re-layouts  153 us (23%)
  blocking collectives  92.9 us (14%)
  other arithmetic  40.9 us (6%)
  starting transfers between devices  31.1 us (5%)
  between operations  14.6 us (2%)
  matrix products  14.5 us (2%)
    psum x1, waiting for transfers between devices, body(): lax.psum((proj_local, out_weight_local, in_gain_local, out_gain_local), (...  245 us
    psum x1, blocking collectives, body(): lax.psum((proj_local, out_weight_local, in_gain_local, out_gain_local), (...  72.4 us
    all_to_all x3, waiting for transfers between devices, exchange(): return lax.all_to_all(x, AXES, split_axis=0, concat_axis=0, tiled=True)  61.1 us
    unnamed x34, local copies, waits for them, and re-layouts  31.1 us
    all_to_all x3, starting transfers between devices, exchange(): return lax.all_to_all(x, AXES, split_axis=0, concat_axis=0, tiled=True)  31 us
    all_to_all x7, other arithmetic, exchange(): return lax.all_to_all(x, AXES, split_axis=0, concat_axis=0, tiled=True)  23.7 us
    all_to_all x1, blocking collectives, exchange(): return lax.all_to_all(x, AXES, split_axis=0, concat_axis=0, tiled=True)  20.4 us
    transpose x5, local copies, waits for them, and re-layouts, matrix(): x.reshape(rows, cols, t, t).transpose(0, 2, 1, 3)  20.2 us
  transfers between devices with their start and end apart: 4, of which 4 were waited for; matrix products, arithmetic and copies ran while one was open for 2% of the time, Pallas kernels for 0%

commit v1 on v0

--- a/solution.py
+++ b/solution.py
@@ -110,7 +110,7 @@
     in_gain_local = jnp.sum(dzn * normed, axis=(0, 1))
     d_pair = layer_back(dzn * in_gain, normed, inverse)
     proj_sum, out_weight_sum, in_gain_sum, out_gain_sum = lax.psum(
-        (proj_local, out_weight_local, in_gain_local, out_gain_local), ("row", "col")
+        lax.psum((proj_local, out_weight_local, in_gain_local, out_gain_local), "row"), "col"
     )
     return (
         d_pair,

time: 660 us -> 683 us (1.035)
  waiting for transfers between devices: 306 us -> 337 us
  blocking collectives: 92.9 us -> 84.4 us
    psum x1 -> x2, waiting for transfers between devices: 245 us -> 275 us  [the longest x1 156 us: body(): lax.psum(lax.psum((proj_local, out_weight_local, in_gain_local, out_gain_...]
    psum x1 -> x2, blocking collectives: 72.4 us -> 64 us  [the longest x1 39.8 us: body(): lax.psum(lax.psum((proj_local, out_weight_local, in_gain_local, out_gain_...]
  transfers between devices with their start and end apart: 4 -> 5, of which waited for: 4 -> 5; matrix products, arithmetic and copies ran while one was open for 2% -> 2% of each run, Pallas kernels for 0% -> 0%
where the time goes in v1:
time: 683 us; the launch traced here: 676 us
  waiting for transfers between devices  337 us (49%)
  local copies, waits for them, and re-layouts  153 us (22%)
  blocking collectives  84.4 us (12%)
  other arithmetic  40.9 us (6%)
  starting transfers between devices  31.1 us (5%)
  matrix products  14.6 us (2%)
  between operations  14.6 us (2%)
    psum x1, waiting for transfers between devices, body(): lax.psum(lax.psum((proj_local, out_weight_local, in_gain_local, out_gain_...  156 us
    psum x1, waiting for transfers between devices, body(): lax.psum((proj_local, out_weight_local, in_gain_local, out_gain_local), '...  119 us
    all_to_all x3, waiting for transfers between devices, exchange(): return lax.all_to_all(x, AXES, split_axis=0, concat_axis=0, tiled=True)  61.1 us
    psum x1, blocking collectives, body(): lax.psum(lax.psum((proj_local, out_weight_local, in_gain_local, out_gain_...  39.8 us
    unnamed x34, local copies, waits for them, and re-layouts  31.1 us
    all_to_all x3, starting transfers between devices, exchange(): return lax.all_to_all(x, AXES, split_axis=0, concat_axis=0, tiled=True)  31 us
    psum x1, blocking collectives, body(): lax.psum((proj_local, out_weight_local, in_gain_local, out_gain_local), '...  24.2 us
    all_to_all x7, other arithmetic, exchange(): return lax.all_to_all(x, AXES, split_axis=0, concat_axis=0, tiled=True)  23.7 us
  transfers between devices with their start and end apart: 5, of which 5 were waited for; matrix products, arithmetic and copies ran while one was open for 2% of the time, Pallas kernels for 0%

profile of v1, /device:TPU:1, one launch (start us, length us, event | category | flops | bytes accessed | tf_op | source)
XLA Modules:
  0.0 675.6 jit_solution(1542144916520759817)
XLA Ops:
  28.2 17.0 %all-to-all-start = ((bf16[256,2,1024]{2,1,0:T(2,128)(2,1)}), bf16[256,2,1024]{2,1,0:T(2,128)(2,1)}, u32[]{:S(2)}, u32[]{:S(2)}) async-start(bf16[256,2,1024]{2,1,0:T(2,128)(2,1)} %reshape.165), calls=%async_computation | async-start | bytes 2097152 | tf_op jit(solution)/shard_map/all_to_all | solution.py:25
  45.2 31.4 %all-to-all-done = bf16[256,2,1024]{2,1,0:T(2,128)(2,1)} async-done(((bf16[256,2,1024]{2,1,0:T(2,128)(2,1)}), bf16[256,2,1024]{2,1,0:T(2,128)(2,1)}, u32[]{:S(2)}, u32[]{:S(2)}) %all-to-all-start) | async-done | bytes 1048608 | tf_op jit(solution)/shard_map/all_to_all | solution.py:25
  76.7 7.5 %reshape.166 = bf16[256,1,2048]{2,1,0:T(2,128)(2,1)} reshape(bf16[256,2,1024]{2,1,0:T(2,128)(2,1)} %all-to-all-done) | data formatting | bytes 2097152
  100.9 4.4 copy.69
  123.0 20.4 %all_to_all.44 = bf16[256,2,256]{2,1,0:T(2,128)(2,1)S(1)} all-to-all(bf16[256,2,256]{2,1,0:T(2,128)(2,1)S(1)} %reshape.167), channel_id=1, replica_groups=mesh['row'=16,'col'=16] {'row','col'}, dimensions={0} | all-to-all | bytes 524288 | tf_op jit(solution)/shard_map/all_to_all | solution.py:25
  158.8 4.3 all_to_all.39
  163.2 5.6 reduce.5
  171.0 7.2 %all-to-all-start.2 = ((bf16[256,2,512]{2,1,0:T(2,128)(2,1)}), bf16[256,2,512]{2,1,0:T(2,128)(2,1)}, u32[]{:S(2)}, u32[]{:S(2)}) async-start(bf16[256,2,512]{2,1,0:T(2,128)(2,1)} %reshape.169), calls=%async_computation.2 | async-start | bytes 1048576 | tf_op jit(solution)/shard_map/all_to_all | solution.py:25
  186.1 12.2 %all-to-all-done.2 = bf16[256,2,512]{2,1,0:T(2,128)(2,1)} async-done(((bf16[256,2,512]{2,1,0:T(2,128)(2,1)}), bf16[256,2,512]{2,1,0:T(2,128)(2,1)}, u32[]{:S(2)}, u32[]{:S(2)}) %all-to-all-start.2) | async-done | bytes 524320 | tf_op jit(solution)/shard_map/all_to_all | solution.py:25
  198.3 4.4 reshape.170
  202.7 4.9 reduce.1
  211.4 4.4 copy.80
  219.6 4.1 reshape_reshape.11
  245.6 5.1 reshape.152
  253.7 5.1 reshape.148
  265.6 6.8 %all-to-all-start.3 = ((bf16[256,2,512]{2,1,0:T(2,128)(2,1)}), bf16[256,2,512]{2,1,0:T(2,128)(2,1)}, u32[]{:S(2)}, u32[]{:S(2)}) async-start(bf16[256,2,512]{2,1,0:T(2,128)(2,1)} %reshape.171), calls=%async_computation.3 | async-start | bytes 1048576 | tf_op jit(solution)/shard_map/all_to_all | solution.py:25
  274.6 17.4 %all-to-all-done.3 = bf16[256,2,512]{2,1,0:T(2,128)(2,1)} async-done(((bf16[256,2,512]{2,1,0:T(2,128)(2,1)}), bf16[256,2,512]{2,1,0:T(2,128)(2,1)}, u32[]{:S(2)}, u32[]{:S(2)}) %all-to-all-start.3) | async-done | bytes 524320 | tf_op jit(solution)/shard_map/all_to_all | solution.py:25
  292.1 4.6 reshape.172
  302.9 4.5 copy.85
  311.1 4.5 copy.84
  323.4 24.2 %all-reduce.2 = (f32[128]{0:T(128)S(1)}, f32[128]{0:T(128)S(1)}) all-reduce(f32[128]{0:T(128)S(1)} %get-tuple-element.7, f32[128]{0:T(128)S(1)} %get-tuple-element.5), channel_id=1, replica_groups=mesh['row'=16,'col'=16] {'row'}, use_global_device_ids=true, to_apply=%region_13.14 | all-reduce | flops 256 | bytes 2048 | tf_op jit(solution)/shard_map/psum | solution.py:113
  347.5 39.8 %all-reduce = (f32[128]{0:T(128)S(1)}, f32[128]{0:T(128)S(1)}) all-reduce(f32[128]{0:T(128)S(1)} %get-tuple-element.15, f32[128]{0:T(128)S(1)} %get-tuple-element.16), channel_id=1, replica_groups=mesh['row'=16,'col'=16] {'col'}, use_global_device_ids=true, to_apply=%region_14.15 | all-reduce | flops 256 | bytes 2048 | tf_op jit(solution)/shard_map/psum | solution.py:112
  388.0 119.5 %all-reduce.9.cloned.1.call-done = (f32[128,640]{1,0:T(8,128)}, f32[128,128]{1,0:T(8,128)}) async-done(((f32[128,640]{1,0:T(8,128)}, f32[128,128]{1,0:T(8,128)}), (f32[128,640]{1,0:T(8,128)}, f32[128,128]{1,0:T(8,128)})) %all-reduce.9.cloned.1.call-update) | async-done | bytes 393232 | tf_op jit(solution)/shard_map/psum | solution.py:113
  509.4 155.9 %all-reduce.7.cloned.1.call-done = (f32[128,640]{1,0:T(8,128)}, f32[128,128]{1,0:T(8,128)}) async-done(((f32[128,640]{1,0:T(8,128)}, f32[128,128]{1,0:T(8,128)}), (f32[128,640]{1,0:T(8,128)}, f32[128,128]{1,0:T(8,128)})) %all-reduce.7.cloned.1.call-update) | async-done | bytes 393232 | tf_op jit(solution)/shard_map/psum | solution.py:112
  (107 shorter events, 145.6 us)
Async XLA Ops:
  7.2 3.3 copy-start
  7.2 4.9 copy-start.5
  28.2 48.5 %all-to-all-start = ((bf16[256,2,1024]{2,1,0:T(2,128)(2,1)}), bf16[256,2,1024]{2,1,0:T(2,128)(2,1)}, u32[]{:S(2)}, u32[]{:S(2)}) async-start(bf16[256,2,1024]{2,1,0:T(2,128)(2,1)} %reshape.165), calls=%async_computation | async-start | bytes 2097152 | tf_op jit(solution)/shard_map/all_to_all | solution.py:25
  96.9 13.4 %copy-start.3 = (bf16[512,512]{1,0:T(8,128)(2,1)}, bf16[512,512]{1,0:T(8,128)(2,1)S(1)}, u32[]{:S(2)}) copy-start(bf16[512,512]{1,0:T(8,128)(2,1)S(1)} %reshape.141) | copy-start | bytes 1572868
  148.8 3.3 copy-start.7
  148.8 3.3 copy-start.9
  171.0 27.3 %all-to-all-start.2 = ((bf16[256,2,512]{2,1,0:T(2,128)(2,1)}), bf16[256,2,512]{2,1,0:T(2,128)(2,1)}, u32[]{:S(2)}, u32[]{:S(2)}) async-start(bf16[256,2,512]{2,1,0:T(2,128)(2,1)} %reshape.169), calls=%async_computation.2 | async-start | bytes 1048576 | tf_op jit(solution)/shard_map/all_to_all | solution.py:25
  265.6 26.4 %all-to-all-start.3 = ((bf16[256,2,512]{2,1,0:T(2,128)(2,1)}), bf16[256,2,512]{2,1,0:T(2,128)(2,1)}, u32[]{:S(2)}, u32[]{:S(2)}) async-start(bf16[256,2,512]{2,1,0:T(2,128)(2,1)} %reshape.171), calls=%async_computation.3 | async-start | bytes 1048576 | tf_op jit(solution)/shard_map/all_to_all | solution.py:25
  272.4 235.0 %all-reduce.9.cloned.1.call-start = ((), (), s32[]{:S(2)}) async-start(), calls=%async_computation.5 | async-start | bytes 786432 | tf_op jit(solution)/shard_map/psum | solution.py:113
  317.2 1.0 copy-start.6
  317.4 2.3 copy-start.1
  317.4 2.3 copy-start.8
  318.7 1.1 copy-start.4
  321.2 186.8 %copy-start.2 = (bf16[32,32,128]{2,1,0:T(8,128)(2,1)S(1)}, bf16[32,32,128]{2,1,0:T(8,128)(2,1)}, u32[]{:S(2)}) copy-start(bf16[32,32,128]{2,1,0:T(8,128)(2,1)} %param.7) | copy-start | bytes 786436
  387.4 277.9 %all-reduce.7.cloned.1.call-start = ((), (), s32[]{:S(2)}) async-start(), calls=%async_computation.4 | async-start | bytes 786432 | tf_op jit(solution)/shard_map/psum | solution.py:112
Sparse Core Ops, SparseCore 0:
  387.5 119.8 all-reduce.8
  510.1 155.1 all-reduce.6
